TPU v7x, 32 devices: a whole 2x2x4 slice. The times are simulated.
32 devices in a mesh: row: 8 (over y, x, core), col: 4 (over z).
Axes of the slice: x: 2, y: 2, z: 4, core: 2. Of those that a mesh axis runs over, the one named last changes fastest.
Arguments:
- matrix: float32 [12288, 12288], P('row', 'col'), may hold values from -10 to 10, as said below
- panel: float32 [12288, 64], P('row'), may hold values from -1.12763724 to 1.12763724
Outputs:
- updated: float32 [12288, 12288], P('row', 'col')
- band_block: float32 [64, 64], replicated
Inputs may be any that keep to these rules, and one draw needn't show every extreme that they name: matrix is exactly symmetric.
All inputs are finite; a program needn't handle non-finite values.
Results may differ from a plain program's by a relative error of at most 0.0002.
Values sent between devices are 32-bit elements; how exact they have to be, the bound alone decides.
No kernel may reach another device: no remote copies, remote signals or barrier semaphores. Data moves between devices by JAX's collectives and lax.ppermute only.
A program may use at most 128 MiB of HBM per device.

v0:
```python
import jax
import jax.numpy as jnp
from jax import lax
from jax.sharding import PartitionSpec as P

precise = lax.Precision.HIGHEST


def upper_cholesky(gram_block):
    order_now = gram_block.shape[0]
    positions = jnp.arange(order_now)

    def one_column(column_index, lower_part):
        gram_column = lax.dynamic_slice_in_dim(gram_block, column_index, 1, 1)[:, 0]
        lower_row = lax.dynamic_slice_in_dim(lower_part, column_index, 1, 0)[0]
        earlier = jnp.where(positions < column_index, lower_row, 0.0)
        reduced = gram_column - jnp.dot(lower_part, earlier, precision=precise)
        pivot_value = jnp.sum(jnp.where(positions == column_index, reduced, 0.0))
        diagonal_value = jnp.sqrt(pivot_value)
        new_column = jnp.where(positions > column_index, reduced / diagonal_value, 0.0) + jnp.where(
            positions == column_index, diagonal_value, 0.0
        )
        return jnp.where(positions[None, :] == column_index, new_column[:, None], lower_part)

    lower_part = lax.fori_loop(
        0, order_now, one_column, jnp.zeros((order_now, order_now), jnp.float32)
    )
    return lower_part.T


def upper_inverse(upper_block):
    order_now = upper_block.shape[0]
    positions = jnp.arange(order_now)

    def one_row(step_count, inverse_part):
        row_at = order_now - 1 - step_count
        upper_row = lax.dynamic_slice_in_dim(upper_block, row_at, 1, 0)[0]
        diagonal_value = jnp.sum(jnp.where(positions == row_at, upper_row, 0.0))
        beyond = jnp.where(positions > row_at, upper_row, 0.0)
        unit_row = jnp.where(positions == row_at, 1.0, 0.0)
        new_row = (unit_row - jnp.dot(beyond, inverse_part, precision=precise)) / diagonal_value
        return jnp.where(positions[:, None] == row_at, new_row[None, :], inverse_part)

    return lax.fori_loop(0, order_now, one_row, jnp.zeros((order_now, order_now), jnp.float32))


def small_factor(block_in):
    order_now = block_in.shape[0]
    positions = jnp.arange(order_now)

    def one_pivot(pivot_index, state_pair):
        working, lower_whole = state_pair
        pivot_column = lax.dynamic_slice_in_dim(working, pivot_index, 1, 1)[:, 0]
        pivot_row = lax.dynamic_slice_in_dim(working, pivot_index, 1, 0)[0]
        pivot_value = jnp.sum(jnp.where(positions == pivot_index, pivot_column, 0.0))
        multipliers = jnp.where(positions > pivot_index, pivot_column / pivot_value, 0.0)
        lower_whole = lower_whole + multipliers[:, None] * (
            positions[None, :] == pivot_index
        ).astype(jnp.float32)
        working = working - multipliers[:, None] * pivot_row[None, :]
        return (working, lower_whole)

    working, lower_whole = lax.fori_loop(
        0, order_now, one_pivot, (block_in, jnp.eye(order_now, dtype=jnp.float32))
    )
    return (lower_whole, jnp.triu(working))


def body(matrix, panel):
    local_rows, local_columns = matrix.shape
    panel_width = panel.shape[1]
    row_index = lax.axis_index("row")
    current_column_index = lax.axis_index("col")
    local_inner = jnp.dot(panel.T, panel, precision=precise)
    head_rows = panel[:panel_width]
    masked = jnp.where(row_index == 0, head_rows, 0.0)
    total_inner, head_rows = lax.psum((local_inner, masked), "row")
    band_factor = -upper_cholesky(total_inner)
    factor_inverse = upper_inverse(band_factor)
    orthogonal_rows = jnp.dot(panel, factor_inverse, precision=precise)
    orthogonal_head = jnp.dot(head_rows, factor_inverse, precision=precise)
    identity = jnp.eye(panel_width, dtype=jnp.float32)
    lower_whole, upper_whole = small_factor(orthogonal_head - identity)
    global_rows = row_index * local_rows + jnp.arange(local_rows)
    unit_rows = (global_rows[:, None] == jnp.arange(panel_width)[None, :]).astype(jnp.float32)
    reflect_rows = jnp.dot(
        orthogonal_rows - unit_rows, upper_inverse(upper_whole), precision=precise
    )
    triangle = -jnp.dot(upper_whole, upper_inverse(lower_whole.T), precision=precise)
    gathered_reflect = lax.all_gather(reflect_rows, "row", axis=0, tiled=True)
    reflect_columns = lax.dynamic_slice_in_dim(
        gathered_reflect, current_column_index * local_columns, local_columns, 0
    )
    partial_product = lax.dot_general(
        matrix, reflect_rows, (((0,), (0,)), ((), ())), precision=precise
    )
    product = lax.psum(partial_product, "row")
    applied_cols = jnp.dot(product, triangle, precision=precise)
    inner_part = jnp.dot(reflect_columns.T, applied_cols, precision=precise)
    inner_total = lax.psum(inner_part, "col")
    coupling = jnp.dot(triangle.T, inner_total, precision=precise)
    corrected_cols = applied_cols - 0.5 * jnp.dot(reflect_columns, coupling, precision=precise)
    gathered_corrected = lax.all_gather(corrected_cols, "col", axis=0, tiled=True)
    corrected_rows = lax.dynamic_slice_in_dim(
        gathered_corrected, row_index * local_rows, local_rows, 0
    )
    left_factor = jnp.concatenate([reflect_rows, corrected_rows], 1)
    right_factor = jnp.concatenate([corrected_cols, reflect_columns], 1)
    updated = matrix - lax.dot_general(
        left_factor, right_factor, (((1,), (1,)), ((), ())), precision=precise
    )
    return (updated, band_factor)


def solution(mesh):
    return jax.shard_map(
        body,
        mesh=mesh,
        in_specs=(P("row", "col"), P("row", None)),
        out_specs=(P("row", "col"), P()),
        check_vma=False,
    )
```

profile of v0, /device:TPU:0, one launch (start us, length us, event | category | flops | bytes accessed | tf_op | source)
XLA Modules:
  0.0 656.6 jit_solution(17921866801268675758)
XLA Ops:
  7.2 1.6 fusion.69
  9.8 26.1 %all-reduce = (f32[64,64]{1,0:T(8,128)S(1)}, f32[64,64]{1,0:T(8,128)S(1)}) all-reduce(f32[64,64]{1,0:T(8,128)S(1)} %fusion.69, f32[64,64]{1,0:T(8,128)S(1)} %broadcast_select_fusion.2), channel_id=1, replica_groups=mesh['row'=8,'col'=4] {'row'}, use_global_device_ids=true, to_apply=%region_0.1 | all-reduce | flops 8192 | bytes 65536 | tf_op jit(solution)/shard_map/psum | solution.py:77
  36.0 102.3 %while.84 = (s32[]{:T(128)}, f32[64,64]{1,0:T(8,128)S(1)}, f32[64,64]{0,1:T(8,128)S(1)}, s32[]{:T(128)}, s32[]{:T(128)}) while((s32[]{:T(128)}, f32[64,64]{1,0:T(8,128)S(1)}, f32[64,64]{0,1:T(8,128)S(1)}, s32[]{:T(128)}, s32[]{:T(128)}) %tuple.192), condition=%wide.region_3.4_spmd.clone.clone, body=%wide.region_1.0_spmd.clone.clone.sunk | while | flops 62274 | bytes 102632 | solution.py:25
  36.1 0.8 select_reduce_fusion.2
  40.8 0.8 select_reduce_fusion.2
  42.4 0.8 select_reduce_fusion.2
  47.2 0.8 select_reduce_fusion.2
  53.6 0.8 select_reduce_fusion.2
  60.0 0.8 select_reduce_fusion.2
  66.4 0.8 select_reduce_fusion.2
  71.2 0.8 select_reduce_fusion.2
  138.4 95.1 %while.85 = (s32[]{:T(128)}, f32[64,64]{1,0:T(8,128)S(1)}, f32[64,64]{1,0:T(8,128)S(1)}, s32[]{:T(128)}, s32[]{:T(128)}, /*index=5*/s32[]{:T(128)}, s32[]{:T(128)}) while((s32[]{:T(128)}, f32[64,64]{1,0:T(8,128)S(1)}, f32[64,64]{1,0:T(8,128)S(1)}, s32[]{:T(128)}, s32[]{:T(128)}, /*index=5*/s32[]{:T(128)}, ...), condition=%wide.region_6.7_spmd.clone.clone, body=%wide.region_4.6_spmd.clone.clone.sunk | while | flops 62086 | bytes 69153 | solution.py:44
  233.7 100.6 %while.83 = (s32[]{:T(128)}, f32[64,64]{0,1:T(8,128)S(1)}, f32[64,64]{0,1:T(8,128)S(1)}, s32[]{:T(128)}) while((s32[]{:T(128)}, f32[64,64]{0,1:T(8,128)S(1)}, f32[64,64]{0,1:T(8,128)S(1)}, s32[]{:T(128)}) %tuple.198), condition=%wide.region_10.11_spmd.clone.clone, body=%wide.region_8.10_spmd.clone.clone.sunk | while | flops 16897 | bytes 69965 | solution.py:63
  334.5 95.1 %while.86 = (s32[]{:T(128)}, f32[64,64]{1,0:T(8,128)S(1)}, f32[64,64]{1,0:T(8,128)S(1)}, s32[]{:T(128)}, s32[]{:T(128)}, /*index=5*/s32[]{:T(128)}, s32[]{:T(128)}) while((s32[]{:T(128)}, f32[64,64]{1,0:T(8,128)S(1)}, f32[64,64]{1,0:T(8,128)S(1)}, s32[]{:T(128)}, s32[]{:T(128)}, /*index=5*/s32[]{:T(128)}, ...), condition=%wide.region_13.14_spmd.clone.clone, body=%wide.region_11.13_spmd.clone.clone.sunk | while | flops 62086 | bytes 69153 | solution.py:44
  429.6 1.5 fusion.59
  431.7 15.5 %convolution_bitcast_fusion.4 = f32[3072,64]{0,1:T(8,128)} fusion(f32[1536,64]{0,1:T(8,128)S(1)} %fusion.70, f32[1536,3072]{1,0:T(8,128)} %param.12), kind=kOutput, calls=%fused_computation.84 | convolution fusion | flops 3623878656 | bytes 20054016 | tf_op jit(solution)/shard_map/dot_general | solution.py:94
  448.0 94.6 %while.87 = (s32[]{:T(128)}, f32[64,64]{1,0:T(8,128)S(1)}, f32[64,64]{1,0:T(8,128)S(1)}, s32[]{:T(128)}, s32[]{:T(128)}, /*index=5*/s32[]{:T(128)}, s32[]{:T(128)}) while((s32[]{:T(128)}, f32[64,64]{1,0:T(8,128)S(1)}, f32[64,64]{1,0:T(8,128)S(1)}, s32[]{:T(128)}, s32[]{:T(128)}, /*index=5*/s32[]{:T(128)}, ...), condition=%wide.region_17.18_spmd.clone.clone, body=%wide.region_15.17_spmd.clone.clone.sunk | while | flops 62086 | bytes 69153 | solution.py:44
  542.8 2.0 fusion.71
  544.8 1.2 constant_dynamic-slice_fusion.8
  546.8 19.3 %psum.31 = f32[64,64]{1,0:T(8,128)S(1)} all-reduce(f32[64,64]{1,0:T(8,128)S(1)} %fusion.72), channel_id=1, replica_groups=mesh['row'=8,'col'=4] {'col'}, use_global_device_ids=true, to_apply=%region_18.19 | all-reduce | flops 4096 | bytes 32768 | tf_op jit(solution)/shard_map/psum | solution.py:100
  566.3 1.7 fusion.58
  568.0 60.0 %all-gather.5.cloned.1.call-done = f32[12288,64]{0,1:T(8,128)} async-done(((f32[3072,64]{0,1:T(8,128)}), f32[12288,64]{0,1:T(8,128)}) %all-gather.5.cloned.1.call-update) | async-done | bytes 3145744 | tf_op jit(solution)/shard_map/all_gather | solution.py:103
  628.0 1.0 constant_dynamic-slice_fusion.7
  629.0 21.1 %convolution_subtract_fusion = f32[1536,3072]{1,0:T(8,128)} fusion(f32[1536,3072]{1,0:T(8,128)} %param.12, f32[3072,64]{0,1:T(8,128)S(1)} %constant_dynamic-slice_fusion.8, f32[3072,64]{0,1:T(8,128)} %fusion.58, f32[1536,64]{0,1:T(8,128)S(1)} %constant_dynamic-slice_fusion.7, f32[1536,64]{0,1:T(8,128)} %copy-done), kind=kOutput, calls=%fused_computation.81 | convolution fusion | flops 7253065728 | bytes 40108032 | tf_op jit(solution)/shard_map/dot_general | solution.py:109
  (1434 shorter events, 436.7 us)
Async XLA Ops:
  7.2 535.6 %all-reduce.3.cloned.1.call-start = ((), (), s32[]{:S(2)}) async-start(), calls=%async_computation | async-start | bytes 1572864 | tf_op jit(solution)/shard_map/psum | solution.py:97
  233.5 416.6 %copy-start.1 = (f32[64,64]{1,0:T(8,128)}, f32[64,64]{1,0:T(8,128)S(1)}, u32[]{:S(2)}) copy-start(f32[64,64]{1,0:T(8,128)S(1)} %get-tuple-element.894) | copy-start | bytes 49156
  431.7 15.6 %copy-start = (f32[1536,64]{0,1:T(8,128)}, f32[1536,64]{0,1:T(8,128)S(1)}, u32[]{:S(2)}) copy-start(f32[1536,64]{0,1:T(8,128)S(1)} %fusion.70) | copy-start | bytes 1179652
  447.2 97.6 %all-gather.3.cloned.1.call-start = ((), (), s32[]{:S(2)}) async-start(), calls=%async_computation.1 | async-start | bytes 3538944 | tf_op jit(solution)/shard_map/all_gather | solution.py:90
  448.0 180.0 %all-gather.5.cloned.1.call-start = ((), (), s32[]{:S(2)}) async-start(), calls=%async_computation.2 | async-start | bytes 3932160 | tf_op jit(solution)/shard_map/all_gather | solution.py:103
Sparse Core Ops, SparseCore 0:
  447.3 55.3 all-reduce.2
  504.6 31.5 all-gather.2
  568.1 59.7 all-gather.4
where the time goes:
time: 660 us; the launch traced here: 657 us
  matrix products  245 us (37%)
  other arithmetic  228 us (35%)
  waiting for transfers between devices  60.7 us (9%)
  loops' own time  48.6 us (7%)
  blocking collectives  45.3 us (7%)
  local copies, waits for them, and re-layouts  14.7 us (2%)
  between operations  14 us (2%)
    dot_general x192, matrix products, one_row(): jnp.dot(beyond, inverse_part, precision=precise)  148 us
    reduce_sum x192, other arithmetic, one_row(): diagonal_value = jnp.sum(jnp.where(positions == row_at, upper_row, 0.0))  120 us
    all_gather x1, waiting for transfers between devices, body(): lax.all_gather(corrected_cols, 'col', axis=0, tiled=True)  60 us
    dot_general x64, matrix products, one_column(): reduced = gram_column - jnp.dot(lower_part, earlier, precision=precise)  51.2 us
    another operation x1, loops' own time, upper_cholesky(): lax.fori_loop(0, order_now, one_column, jnp.zeros((order_now, order_now),...  45 us
    mul x64, other arithmetic, one_pivot(): working = working - multipliers[:, None] * pivot_row[None, :]  41.9 us
    reduce_sum x64, other arithmetic, one_pivot(): jnp.sum(jnp.where(positions == pivot_index, pivot_column, 0.0))  38.8 us
    psum x1, blocking collectives, body(): total_inner, head_rows = lax.psum((local_inner, masked), 'row')  26.1 us
  transfers between devices with their start and end apart: 3, of which 1 were waited for; matrix products, arithmetic and copies ran while one was open for 15% of the time, Pallas kernels for 0%

commit v1 on v0

--- a/solution.py
+++ b/solution.py
@@ -100,7 +100,16 @@
     inner_total = lax.psum(inner_part, "col")
     coupling = jnp.dot(triangle.T, inner_total, precision=precise)
     corrected_cols = applied_cols - 0.5 * jnp.dot(reflect_columns, coupling, precision=precise)
-    gathered_corrected = lax.all_gather(corrected_cols, "col", axis=0, tiled=True)
+
+    def draw_the_zone(mat):
+        return jnp.concatenate(
+            jax.lax.all_to_all(
+                jnp.stack([mat for _ in range(jax.lax.axis_size("col"))]), "col", 0, 0
+            ),
+            axis=0,
+        )
+
+    gathered_corrected = draw_the_zone(corrected_cols)
     corrected_rows = lax.dynamic_slice_in_dim(
         gathered_corrected, row_index * local_rows, local_rows, 0
     )

time: 660 us -> 670 us (1.015)
    all_to_all x0 -> x1, waiting for transfers between devices: none -> 64.5 us  [draw_the_zone(): jax.lax.all_to_all(jnp.stack([mat for _ in range(jax.lax.axis_size('col')...]
    all_gather x1 -> x0, waiting for transfers between devices: 60 us -> none  [body(): lax.all_gather(corrected_cols, 'col', axis=0, tiled=True)]
  transfers between devices with their start and end apart: 3 -> 3, of which waited for: 1 -> 1; matrix products, arithmetic and copies ran while one was open for 15% -> 14% of each run, Pallas kernels for 0% -> 0%
where the time goes in v1:
time: 670 us; the launch traced here: 667 us
  matrix products  242 us (36%)
  other arithmetic  228 us (34%)
  waiting for transfers between devices  65.2 us (10%)
  loops' own time  48.6 us (7%)
  blocking collectives  45.3 us (7%)
  local copies, waits for them, and re-layouts  18.7 us (3%)
  between operations  14.3 us (2%)
    dot_general x192, matrix products, one_row(): jnp.dot(beyond, inverse_part, precision=precise)  148 us
    reduce_sum x192, other arithmetic, one_row(): diagonal_value = jnp.sum(jnp.where(positions == row_at, upper_row, 0.0))  120 us
    all_to_all x1, waiting for transfers between devices, draw_the_zone(): jax.lax.all_to_all(jnp.stack([mat for _ in range(jax.lax.axis_size('col')...  64.5 us
    dot_general x64, matrix products, one_column(): reduced = gram_column - jnp.dot(lower_part, earlier, precision=precise)  51.2 us
    another operation x1, loops' own time, upper_cholesky(): lax.fori_loop(0, order_now, one_column, jnp.zeros((order_now, order_now),...  45 us
    mul x64, other arithmetic, one_pivot(): working = working - multipliers[:, None] * pivot_row[None, :]  41.9 us
    reduce_sum x64, other arithmetic, one_pivot(): jnp.sum(jnp.where(positions == pivot_index, pivot_column, 0.0))  38.8 us
    psum x1, blocking collectives, body(): total_inner, head_rows = lax.psum((local_inner, masked), 'row')  26.1 us
  transfers between devices with their start and end apart: 3, of which 1 were waited for; matrix products, arithmetic and copies ran while one was open for 14% of the time, Pallas kernels for 0%

profile of v1, /device:TPU:0, one launch (start us, length us, event | category | flops | bytes accessed | tf_op | source)
XLA Modules:
  0.0 666.7 jit_solution(12224079568297718163)
XLA Ops:
  7.2 1.7 fusion.69
  9.8 26.1 %all-reduce = (f32[64,64]{1,0:T(8,128)S(1)}, f32[64,64]{1,0:T(8,128)S(1)}) all-reduce(f32[64,64]{1,0:T(8,128)S(1)} %fusion.69, f32[64,64]{1,0:T(8,128)S(1)} %broadcast_select_fusion.2), channel_id=1, replica_groups=mesh['row'=8,'col'=4] {'row'}, use_global_device_ids=true, to_apply=%region_0.1 | all-reduce | flops 8192 | bytes 65536 | tf_op jit(solution)/shard_map/psum | solution.py:77
  36.0 102.2 %while.84 = (s32[]{:T(128)}, f32[64,64]{1,0:T(8,128)S(1)}, f32[64,64]{0,1:T(8,128)S(1)}, s32[]{:T(128)}, s32[]{:T(128)}) while((s32[]{:T(128)}, f32[64,64]{1,0:T(8,128)S(1)}, f32[64,64]{0,1:T(8,128)S(1)}, s32[]{:T(128)}, s32[]{:T(128)}) %tuple.194), condition=%wide.region_3.4_spmd.clone.clone, body=%wide.region_1.0_spmd.clone.clone.sunk | while | flops 62274 | bytes 102632 | solution.py:25
  42.5 0.8 select_reduce_fusion.2
  45.7 0.8 select_reduce_fusion.2
  53.7 0.8 select_reduce_fusion.2
  56.8 0.8 select_reduce_fusion.2
  61.6 0.8 select_reduce_fusion.2
  64.8 0.8 select_reduce_fusion.2
  138.4 95.1 %while.85 = (s32[]{:T(128)}, f32[64,64]{1,0:T(8,128)S(1)}, f32[64,64]{1,0:T(8,128)S(1)}, s32[]{:T(128)}, s32[]{:T(128)}, /*index=5*/s32[]{:T(128)}, s32[]{:T(128)}) while((s32[]{:T(128)}, f32[64,64]{1,0:T(8,128)S(1)}, f32[64,64]{1,0:T(8,128)S(1)}, s32[]{:T(128)}, s32[]{:T(128)}, /*index=5*/s32[]{:T(128)}, ...), condition=%wide.region_6.7_spmd.clone.clone, body=%wide.region_4.6_spmd.clone.clone.sunk | while | flops 62086 | bytes 69153 | solution.py:44
  234.3 100.6 %while.83 = (s32[]{:T(128)}, f32[64,64]{0,1:T(8,128)S(1)}, f32[64,64]{0,1:T(8,128)S(1)}, s32[]{:T(128)}) while((s32[]{:T(128)}, f32[64,64]{0,1:T(8,128)S(1)}, f32[64,64]{0,1:T(8,128)S(1)}, s32[]{:T(128)}) %tuple.200), condition=%wide.region_10.11_spmd.clone.clone, body=%wide.region_8.10_spmd.clone.clone.sunk | while | flops 16897 | bytes 69965 | solution.py:63
  335.1 95.1 %while.86 = (s32[]{:T(128)}, f32[64,64]{1,0:T(8,128)S(1)}, f32[64,64]{1,0:T(8,128)S(1)}, s32[]{:T(128)}, s32[]{:T(128)}, /*index=5*/s32[]{:T(128)}, s32[]{:T(128)}) while((s32[]{:T(128)}, f32[64,64]{1,0:T(8,128)S(1)}, f32[64,64]{1,0:T(8,128)S(1)}, s32[]{:T(128)}, s32[]{:T(128)}, /*index=5*/s32[]{:T(128)}, ...), condition=%wide.region_13.14_spmd.clone.clone, body=%wide.region_11.13_spmd.clone.clone.sunk | while | flops 62086 | bytes 69153 | solution.py:44
  431.3 15.5 %convolution_bitcast_fusion.4 = f32[3072,64]{0,1:T(8,128)} fusion(f32[1536,64]{0,1:T(8,128)S(1)} %fusion.70, f32[1536,3072]{1,0:T(8,128)} %param.12), kind=kOutput, calls=%fused_computation.84 | convolution fusion | flops 3623878656 | bytes 20054016 | tf_op jit(solution)/shard_map/dot_general | solution.py:94
  447.6 94.6 %while.87 = (s32[]{:T(128)}, f32[64,64]{1,0:T(8,128)S(1)}, f32[64,64]{1,0:T(8,128)S(1)}, s32[]{:T(128)}, s32[]{:T(128)}, /*index=5*/s32[]{:T(128)}, s32[]{:T(128)}) while((s32[]{:T(128)}, f32[64,64]{1,0:T(8,128)S(1)}, f32[64,64]{1,0:T(8,128)S(1)}, s32[]{:T(128)}, s32[]{:T(128)}, /*index=5*/s32[]{:T(128)}, ...), condition=%wide.region_17.18_spmd.clone.clone, body=%wide.region_15.17_spmd.clone.clone.sunk | while | flops 62086 | bytes 69153 | solution.py:44
  542.4 2.0 fusion.71
  544.4 1.2 constant_dynamic-slice_fusion.8
  546.3 19.2 %psum.31 = f32[64,64]{1,0:T(8,128)S(1)} all-reduce(f32[64,64]{1,0:T(8,128)S(1)} %fusion.72), channel_id=1, replica_groups=mesh['row'=8,'col'=4] {'col'}, use_global_device_ids=true, to_apply=%region_18.19 | all-reduce | flops 4096 | bytes 32768 | tf_op jit(solution)/shard_map/psum | solution.py:100
  565.8 0.8 fusion.58
  566.7 0.9 copy-done.2
  567.6 2.0 stack.2
  569.6 3.9 all-to-all-start
  573.5 64.5 %all-to-all-done = f32[4,3072,64]{1,2,0:T(8,128)S(1)} async-done(((f32[4,3072,64]{1,2,0:T(8,128)}), f32[4,3072,64]{1,2,0:T(8,128)S(1)}, u32[]{:S(2)}, u32[]{:S(2)}) %all-to-all-start) | async-done | bytes 3145760 | tf_op jit(solution)/shard_map/all_to_all | solution.py:106
  638.2 0.9 copy-done.1
  639.5 20.4 %convolution_subtract_fusion = f32[1536,3072]{1,0:T(8,128)} fusion(f32[1536,3072]{1,0:T(8,128)} %param.12, f32[3072,64]{0,1:T(8,128)S(1)} %copy-done.1, f32[3072,64]{0,1:T(8,128)S(1)} %copy-done.3, f32[1536,64]{0,1:T(8,128)S(1)} %constant_dynamic-slice_fusion.7, f32[1536,64]{0,1:T(8,128)S(1)} %copy-done.5), kind=kOutput, calls=%fused_computation.81 | convolution fusion | flops 7253065728 | bytes 40108032 | tf_op jit(solution)/shard_map/dot_general | solution.py:118
  (1447 shorter events, 440.0 us)
Async XLA Ops:
  7.2 423.0 %copy-start.6 = (f32[1536,64]{0,1:T(8,128)S(1)}, f32[1536,64]{0,1:T(8,128)}, u32[]{:S(2)}) copy-start(f32[1536,64]{0,1:T(8,128)} %param.13) | copy-start | bytes 1179652
  7.2 535.2 %all-reduce.3.cloned.1.call-start = ((), (), s32[]{:S(2)}) async-start(), calls=%async_computation.1 | async-start | bytes 1572864 | tf_op jit(solution)/shard_map/psum | solution.py:97
  233.5 0.6 copy-start.7
  431.3 15.5 %copy-start.4 = (f32[1536,64]{0,1:T(8,128)}, f32[1536,64]{0,1:T(8,128)S(1)}, u32[]{:S(2)}) copy-start(f32[1536,64]{0,1:T(8,128)S(1)} %fusion.70) | copy-start | bytes 1179652
  446.8 97.5 %all-gather.2.cloned.1.call-start = ((), (), s32[]{:S(2)}) async-start(), calls=%async_computation.2 | async-start | bytes 3538944 | tf_op jit(solution)/shard_map/all_gather | solution.py:90
  545.5 24.1 %copy-start = (f32[3072,64]{0,1:T(8,128)}, f32[3072,64]{0,1:T(8,128)S(1)}, u32[]{:S(2)}) copy-start(f32[3072,64]{0,1:T(8,128)S(1)} %constant_dynamic-slice_fusion.8) | copy-start | bytes 2359300
  566.7 0.9 copy-start.2
  569.6 68.4 %all-to-all-start = ((f32[4,3072,64]{1,2,0:T(8,128)}), f32[4,3072,64]{1,2,0:T(8,128)S(1)}, u32[]{:S(2)}, u32[]{:S(2)}) async-start(f32[4,3072,64]{1,2,0:T(8,128)} %stack.2), calls=%async_computation | async-start | bytes 6291456 | tf_op jit(solution)/shard_map/all_to_all | solution.py:106
  638.0 1.1 copy-start.1
  638.0 1.4 copy-start.3
  638.0 1.5 copy-start.5
Sparse Core Ops, SparseCore 0:
  446.9 55.2 all-reduce.2
  504.2 31.5 all-gather.1
